TPU v7x, 128 devices: a whole 4x4x4 slice. The times are simulated.
128 devices in a mesh: wide: 16 (over z, x), narrow: 8 (over y, core).
Axes of the slice: x: 4, y: 4, z: 4, core: 2. Of those that a mesh axis runs over, the one named last changes fastest.
Arguments:
- inputs: bfloat16 [4, 256, 16384], P(None, 'wide', 'narrow'), may hold values from -600 to 600
- norm_gain: bfloat16 [16384], P('narrow'), may hold values from 0.099609375 to 1.8984375
- w_query: bfloat16 [16384, 8192], P('narrow', 'wide'), may hold values from -0.0234375 to 0.0234375
- w_keyval: bfloat16 [16384, 1024], P('narrow', 'wide'), may hold values from -0.0234375 to 0.0234375
- w_out: bfloat16 [8192, 16384], P('wide', 'narrow'), may hold values from -0.0625 to 0.0625
- key_cache: bfloat16 [256, 4096, 512], P(('wide', 'narrow')), may hold values from -1700 to 1700
- value_cache: bfloat16 [256, 4096, 512], P(('wide', 'narrow')), may hold values from -48 to 48
- lengths: int32 [256], P(('wide', 'narrow')), may hold values from 1024 to 4092, as said below
- positions: int32 [256], P(('wide', 'narrow')), may hold values from 1024 to 8187, as said below
Outputs:
- attended: bfloat16 [4, 256, 16384], P(None, 'wide', 'narrow')
- new_keys: bfloat16 [4, 256, 512], P(None, ('wide', 'narrow'))
- new_values: bfloat16 [4, 256, 512], P(None, ('wide', 'narrow'))
Inputs may be any that keep to these rules, and one draw needn't show every extreme that they name: A row's cache holds its first lengths slots. `positions`: a row's later new tokens follow its first one position by position.
All inputs are finite; a program needn't handle non-finite values.
Results may differ from a plain program's by a relative error of at most 0.007.
The roundings to bfloat16 on the way count: a program that leaves them out, or rounds other values in their place, can miss the bound.
Values may be sent and summed in bfloat16 or wider, within the bound.
A program may use at most 128 MiB of HBM per device.

v0:
```python
import jax
import jax.numpy as jnp
from jax import lax
from jax.sharding import PartitionSpec as P

D = 16384
HQ = 64
KVH = 4
HD = 128
STEPS = 4


def rotate(values, rotary_pos):
    half_dim = values.shape[-1] // 2
    inverse_freq = jnp.exp(
        -jnp.log(jnp.float32(500000.0))
        * jnp.arange(half_dim, dtype=jnp.float32)
        * 2.0
        / (2 * half_dim)
    )
    angles = rotary_pos.astype(jnp.float32)[..., None] * inverse_freq
    cosine = jnp.cos(angles)[..., None, :]
    sine = jnp.sin(angles)[..., None, :]
    first_half = values[..., :half_dim]
    second_half = values[..., half_dim:]
    return jnp.concatenate(
        [first_half * cosine - second_half * sine, second_half * cosine + first_half * sine],
        axis=-1,
    )


def local(inputs, norm_gain, w_query, w_keyval, w_out, key_cache, value_cache, lengths, positions):
    wide_count = lax.axis_size("wide")
    narrow_count = lax.axis_size("narrow")
    rows_dev = key_cache.shape[0]
    cache_len = key_cache.shape[1]
    q_local = w_query.shape[1]
    kv_local = w_keyval.shape[1]
    col_count = q_local + kv_local
    group_size = HQ // KVH
    factor = 1.0 / jnp.sqrt(jnp.float32(HD))
    step_outputs = []
    key_list = []
    value_list = []
    for step_index in range(STEPS):
        prepare_step_block = inputs[step_index : step_index + 1]
        project_count_steps = prepare_step_block.shape[0]
        row_values = prepare_step_block.astype(jnp.float32)
        partial_square = jnp.sum(row_values * row_values, axis=-1)
        total_square = lax.psum(partial_square, "narrow")
        inv_rms = lax.rsqrt(total_square / D + 1e-05)
        normed = (row_values * inv_rms[..., None] * norm_gain.astype(jnp.float32)).astype(
            jnp.bfloat16
        )
        shard_piece = lax.all_gather(normed, "wide", axis=1, tiled=True)
        first_part = jnp.einsum(
            "trd,dc->trc", shard_piece, w_query, preferred_element_type=jnp.float32
        )
        second_part = jnp.einsum(
            "trd,dc->trc", shard_piece, w_keyval, preferred_element_type=jnp.float32
        )
        project_partials = jnp.concatenate([first_part, second_part], axis=2)
        split_terms = project_partials.reshape(
            project_count_steps, wide_count, narrow_count, rows_dev, col_count
        )
        summed = lax.psum_scatter(split_terms, "narrow", scatter_dimension=2, tiled=True).astype(
            jnp.bfloat16
        )
        summed = summed.reshape(project_count_steps, wide_count, rows_dev, col_count)
        received = lax.all_to_all(summed, "wide", split_axis=1, concat_axis=3, tiled=True)
        arranged = received.reshape(project_count_steps, rows_dev, wide_count, col_count)
        query = arranged[..., :q_local].reshape(project_count_steps, rows_dev, HQ * HD)
        keyval = arranged[..., q_local:].reshape(project_count_steps, rows_dev, 2 * KVH * HD)
        prepare_count_steps = prepare_step_block.shape[0]
        rotary_pos = (
            positions[None, :]
            + step_index
            + jnp.arange(prepare_count_steps, dtype=jnp.int32)[:, None]
        )
        prepare_rot_query = rotate(
            query.astype(jnp.float32).reshape(prepare_count_steps, rows_dev, HQ, HD), rotary_pos
        )
        prepare_rot_query = prepare_rot_query.astype(jnp.bfloat16).reshape(
            prepare_count_steps, rows_dev, HQ * HD
        )
        rot_keys = rotate(
            keyval[..., : KVH * HD]
            .astype(jnp.float32)
            .reshape(prepare_count_steps, rows_dev, KVH, HD),
            rotary_pos,
        )
        rot_keys = rot_keys.astype(jnp.bfloat16).reshape(prepare_count_steps, rows_dev, KVH * HD)
        rot_query, rot_keys, new_vals = (prepare_rot_query, rot_keys, keyval[..., KVH * HD :])
        key_list.append(rot_keys)
        value_list.append(new_vals)
        fresh_keys = jnp.concatenate(key_list, axis=0)
        attend_count_steps = rot_query.shape[0]
        fresh_count = fresh_keys.shape[0]
        grouped = rot_query.reshape(attend_count_steps, rows_dev, KVH, group_size, HD)
        cached = key_cache.reshape(rows_dev, cache_len, KVH, HD)
        cache_scores = (
            jnp.einsum("trgqd,rsgd->rgtqs", grouped, cached, preferred_element_type=jnp.float32)
            * factor
        )
        visible = jnp.arange(cache_len, dtype=jnp.int32)[None, :] < lengths[:, None]
        cache_scores = jnp.where(visible[:, None, None, None, :], cache_scores, -jnp.inf)
        fresh_view = fresh_keys.reshape(fresh_count, rows_dev, KVH, HD)
        fresh_scores = (
            jnp.einsum("trgqd,jrgd->rgtqj", grouped, fresh_view, preferred_element_type=jnp.float32)
            * factor
        )
        causal_mask = (
            jnp.arange(fresh_count, dtype=jnp.int32)[None, :]
            <= (step_index + jnp.arange(attend_count_steps, dtype=jnp.int32))[:, None]
        )
        fresh_scores = jnp.where(causal_mask[None, None, :, None, :], fresh_scores, -jnp.inf)
        highest = jnp.maximum(jnp.max(cache_scores, -1), jnp.max(fresh_scores, -1))[..., None]
        cache_exp = jnp.exp(cache_scores - highest)
        fresh_exp = jnp.exp(fresh_scores - highest)
        normaliser = jnp.sum(cache_exp, -1, keepdims=True) + jnp.sum(fresh_exp, -1, keepdims=True)
        cache_weights = (cache_exp / normaliser).astype(jnp.bfloat16)
        fresh_weights = (fresh_exp / normaliser).astype(jnp.bfloat16)
        cached_values = value_cache.reshape(rows_dev, cache_len, KVH, HD)
        fresh_vals = jnp.concatenate(value_list, axis=0).reshape(fresh_count, rows_dev, KVH, HD)
        output = jnp.einsum(
            "rgtqs,rsgd->trgqd", cache_weights, cached_values, preferred_element_type=jnp.float32
        )
        output = output + jnp.einsum(
            "rgtqj,jrgd->trgqd", fresh_weights, fresh_vals, preferred_element_type=jnp.float32
        )
        attended_heads = output.astype(jnp.bfloat16).reshape(attend_count_steps, rows_dev, HQ * HD)
        count_steps = attended_heads.shape[0]
        by_heads = lax.all_to_all(
            attended_heads.reshape(count_steps, 1, rows_dev, HQ * HD),
            "wide",
            split_axis=3,
            concat_axis=1,
            tiled=True,
        )
        by_heads = by_heads.reshape(count_steps, wide_count, 1, rows_dev, by_heads.shape[-1])
        partials = jnp.einsum(
            "twprh,hc->twprc",
            lax.all_gather(by_heads, "narrow", axis=2, tiled=True),
            w_out,
            preferred_element_type=jnp.float32,
        )
        partials = partials.reshape(
            count_steps, wide_count * narrow_count * rows_dev, partials.shape[-1]
        )
        step_outputs.append(
            lax.psum_scatter(partials, "wide", scatter_dimension=1, tiled=True).astype(jnp.bfloat16)
        )
    return (
        jnp.concatenate(step_outputs, axis=0),
        jnp.concatenate(key_list, axis=0),
        jnp.concatenate(value_list, axis=0),
    )


def solution(mesh):
    return jax.shard_map(
        local,
        mesh=mesh,
        in_specs=(
            P(None, "wide", "narrow"),
            P("narrow"),
            P("narrow", "wide"),
            P("narrow", "wide"),
            P("wide", "narrow"),
            P(("wide", "narrow"), None, None),
            P(("wide", "narrow"), None, None),
            P(("wide", "narrow")),
            P(("wide", "narrow")),
        ),
        out_specs=(
            P(None, "wide", "narrow"),
            P(None, ("wide", "narrow"), None),
            P(None, ("wide", "narrow"), None),
        ),
        check_vma=False,
    )
```

profile of v0, /device:TPU:0, one launch (start us, length us, event | category | flops | bytes accessed | tf_op | source)
XLA Modules:
  0.0 833.2 jit_solution(438713747634489099)
XLA Ops:
  9.2 15.0 %all-reduce = (f32[1,16]{1,0:T(1,128)S(1)}, f32[1,16]{1,0:T(1,128)S(1)}, f32[1,16]{1,0:T(1,128)S(1)}, f32[1,16]{1,0:T(1,128)S(1)}) all-reduce(f32[1,16]{1,0:T(1,128)S(1)} %bitcast.378, f32[1,16]{1,0:T(1,128)S(1)} %bitcast.379, f32[1,16]{1,0:T(1,128)S(1)} %bitcast.377, ...), channel_id=1, replica_groups=mesh['wide'=16,'narrow'=8] {'narrow'}, use_global_device_ids=true, to_apply=%region_23.24 | all-reduce | flops 64 | bytes 512 | tf_op jit(solution)/shard_map/psum | solution.py:50
  24.2 1.7 fusion.124
  28.1 40.4 %all-gather.7.cloned.1.call-done = bf16[1,256,2048]{2,1,0:T(8,128)(2,1)} async-done(((bf16[1,16,2048]{2,1,0:T(8,128)(2,1)}), bf16[1,256,2048]{2,1,0:T(8,128)(2,1)}) %all-gather.7.cloned.1.call-update) | async-done | bytes 1048592 | tf_op jit(solution)/shard_map/all_gather | solution.py:55
  68.5 1.7 reshape.1160
  70.7 2.3 fusion.63
  74.2 38.9 %all-gather.5.cloned.1.call-done = bf16[1,256,2048]{2,1,0:T(8,128)(2,1)} async-done(((bf16[1,16,2048]{2,1,0:T(8,128)(2,1)}), bf16[1,256,2048]{2,1,0:T(8,128)(2,1)}) %all-gather.5.cloned.1.call-update) | async-done | bytes 1048592 | tf_op jit(solution)/shard_map/all_gather | solution.py:55
  113.1 1.7 reshape.1150
  115.3 2.3 fusion.60
  119.0 38.2 %all-gather.11.cloned.1.call-done = bf16[1,256,2048]{2,1,0:T(8,128)(2,1)} async-done(((bf16[1,16,2048]{2,1,0:T(8,128)(2,1)}), bf16[1,256,2048]{2,1,0:T(8,128)(2,1)}) %all-gather.11.cloned.1.call-update) | async-done | bytes 1048592 | tf_op jit(solution)/shard_map/all_gather | solution.py:55
  157.2 1.7 reshape.1176
  159.4 2.3 fusion.69
  163.0 38.1 %all-gather.9.cloned.1.call-done = bf16[1,256,2048]{2,1,0:T(8,128)(2,1)} async-done(((bf16[1,16,2048]{2,1,0:T(8,128)(2,1)}), bf16[1,256,2048]{2,1,0:T(8,128)(2,1)}) %all-gather.9.cloned.1.call-update) | async-done | bytes 1048592 | tf_op jit(solution)/shard_map/all_gather | solution.py:55
  201.1 1.7 reshape.1168
  203.3 2.3 fusion.66
  206.7 27.4 %reduce-scatter.13.cloned.1.call-done = f32[1,16,1,2,576]{4,1,3,0,2:T(8,128)} async-done(((f32[1,16,8,2,576]{4,1,3,0,2:T(8,128)}), f32[1,16,1,2,576]{4,1,3,0,2:T(8,128)}) %reduce-scatter.13.cloned.1.call-update) | async-done | bytes 73744 | tf_op jit(solution)/shard_map/reduce_scatter | solution.py:66
  235.7 6.9 all-to-all-start.2
  242.6 24.2 %reduce-scatter.9.cloned.1.call-done = f32[1,16,1,2,576]{4,1,3,0,2:T(8,128)} async-done(((f32[1,16,8,2,576]{4,1,3,0,2:T(8,128)}), f32[1,16,1,2,576]{4,1,3,0,2:T(8,128)}) %reduce-scatter.9.cloned.1.call-update) | async-done | bytes 73744 | tf_op jit(solution)/shard_map/reduce_scatter | solution.py:66
  268.3 7.1 all-to-all-start
  275.7 7.2 all-to-all-done
  283.4 5.8 fusion.189
  289.9 4.8 fusion.75
  295.0 6.8 copy.243
  302.3 46.5 %reduce.42 = bf16[8192,2]{1,0:T(8,128)(2,1)} reduce(bf16[8192,1,1,2]{3,2,1,0:T(2,128)(2,1)} %bitcast.332, bf16[]{:T(256)} %broadcast.355), dimensions={1,2}, to_apply=%bitcast.274.reduce_sub_computation | reduce | bytes 65538
  348.9 4.8 reshape.1213
  353.6 3.5 all-to-all-start.3
  358.7 6.0 all-to-all-done.3
  364.7 3.5 all-to-all-start.6
  368.2 8.4 %reshape.1214 = bf16[8192,1,1,2]{3,2,1,0:T(2,128)(2,1)} reshape(bf16[16,2,512]{2,1,0:T(2,128)(2,1)S(1)} %all-to-all-done.3) | data formatting | bytes 65536
  376.6 8.1 copy.244
  384.7 12.8 %all_gather.27 = bf16[1,16,8,2,512]{4,1,3,0,2:T(8,128)(2,1)S(1)} all-gather(bf16[1,16,1,2,512]{4,1,3,0,2:T(8,128)(2,1)S(1)} %bitcast.368), channel_id=1, replica_groups=mesh['wide'=16,'narrow'=8] {'narrow'}, dimensions={2}, use_global_device_ids=true | all-gather | bytes 294912 | tf_op jit(solution)/shard_map/all_gather | solution.py:143
  398.0 2.0 convolution_bitcast_fusion.2
  401.6 7.2 all-to-all-start.4
  409.4 6.9 all-to-all-done.4
  417.3 5.8 fusion.185
  423.6 4.8 fusion.81
  428.7 6.8 copy.269
  435.4 46.6 %reduce.40 = bf16[8192,2]{1,0:T(8,128)(2,1)} reduce(bf16[8192,1,1,2]{3,2,1,0:T(2,128)(2,1)} %bitcast.335, bf16[]{:T(256)} %broadcast.355), dimensions={1,2}, to_apply=%bitcast.270.reduce_sub_computation | reduce | bytes 65538
  482.0 4.2 reshape.1209
  486.2 10.7 %all_to_all.120 = bf16[16,2,512]{2,1,0:T(2,128)(2,1)S(1)} all-to-all(bf16[16,2,512]{2,1,0:T(2,128)(2,1)S(1)} %reshape.1209), channel_id=1, replica_groups=mesh['wide'=16,'narrow'=8] {'wide'}, dimensions={0} | all-to-all | bytes 65536 | tf_op jit(solution)/shard_map/all_to_all | solution.py:133
  496.9 8.4 %reshape.1210 = bf16[8192,1,1,2]{3,2,1,0:T(2,128)(2,1)} reshape(bf16[16,2,512]{2,1,0:T(2,128)(2,1)S(1)} %all_to_all.120) | data formatting | bytes 65536
  505.3 8.1 copy.270
  513.4 13.0 %all_gather.31 = bf16[1,16,8,2,512]{4,1,3,0,2:T(8,128)(2,1)S(1)} all-gather(bf16[1,16,1,2,512]{4,1,3,0,2:T(8,128)(2,1)S(1)} %bitcast.369), channel_id=1, replica_groups=mesh['wide'=16,'narrow'=8] {'narrow'}, dimensions={2}, use_global_device_ids=true | all-gather | bytes 294912 | tf_op jit(solution)/shard_map/all_gather | solution.py:143
  526.8 2.1 convolution_bitcast_fusion
  529.4 5.8 fusion.187
  535.6 4.8 fusion.78
  540.7 6.8 copy.256
  547.5 46.6 %reduce.41 = bf16[8192,2]{1,0:T(8,128)(2,1)} reduce(bf16[8192,1,1,2]{3,2,1,0:T(2,128)(2,1)} %bitcast.337, bf16[]{:T(256)} %broadcast.355), dimensions={1,2}, to_apply=%bitcast.272.reduce_sub_computation | reduce | bytes 65538
  594.1 4.2 reshape.1211
  598.3 10.8 %all_to_all.121 = bf16[16,2,512]{2,1,0:T(2,128)(2,1)S(1)} all-to-all(bf16[16,2,512]{2,1,0:T(2,128)(2,1)S(1)} %reshape.1211), channel_id=1, replica_groups=mesh['wide'=16,'narrow'=8] {'wide'}, dimensions={0} | all-to-all | bytes 65536 | tf_op jit(solution)/shard_map/all_to_all | solution.py:133
  609.1 8.4 %reshape.1212 = bf16[8192,1,1,2]{3,2,1,0:T(2,128)(2,1)} reshape(bf16[16,2,512]{2,1,0:T(2,128)(2,1)S(1)} %all_to_all.121) | data formatting | bytes 65536
  617.5 8.1 copy.257
  625.6 13.1 %all_gather.29 = bf16[1,16,8,2,512]{4,1,3,0,2:T(8,128)(2,1)S(1)} all-gather(bf16[1,16,1,2,512]{4,1,3,0,2:T(8,128)(2,1)S(1)} %bitcast.370), channel_id=1, replica_groups=mesh['wide'=16,'narrow'=8] {'narrow'}, dimensions={2}, use_global_device_ids=true | all-gather | bytes 294912 | tf_op jit(solution)/shard_map/all_gather | solution.py:143
  639.0 2.1 convolution_bitcast_fusion.1
  641.6 5.8 fusion.191
  647.9 4.8 fusion.96
  652.8 6.8 copy.230
  659.6 46.5 %reduce.43 = bf16[8192,2]{1,0:T(8,128)(2,1)} reduce(bf16[8192,1,1,2]{3,2,1,0:T(2,128)(2,1)} %bitcast.333, bf16[]{:T(256)} %broadcast.355), dimensions={1,2}, to_apply=%bitcast.276.reduce_sub_computation | reduce | bytes 65538
  706.1 4.2 reshape.1215
  710.2 10.8 %all_to_all.122 = bf16[16,2,512]{2,1,0:T(2,128)(2,1)S(1)} all-to-all(bf16[16,2,512]{2,1,0:T(2,128)(2,1)S(1)} %reshape.1215), channel_id=1, replica_groups=mesh['wide'=16,'narrow'=8] {'wide'}, dimensions={0} | all-to-all | bytes 65536 | tf_op jit(solution)/shard_map/all_to_all | solution.py:133
  721.0 8.4 %reshape.1216 = bf16[8192,1,1,2]{3,2,1,0:T(2,128)(2,1)} reshape(bf16[16,2,512]{2,1,0:T(2,128)(2,1)S(1)} %all_to_all.122) | data formatting | bytes 65536
  729.4 8.1 copy.231
  737.5 12.8 %all_gather.25 = bf16[1,16,8,2,512]{4,1,3,0,2:T(8,128)(2,1)S(1)} all-gather(bf16[1,16,1,2,512]{4,1,3,0,2:T(8,128)(2,1)S(1)} %bitcast.371), channel_id=1, replica_groups=mesh['wide'=16,'narrow'=8] {'narrow'}, dimensions={2}, use_global_device_ids=true | all-gather | bytes 294912 | tf_op jit(solution)/shard_map/all_gather | solution.py:143
  750.7 2.1 convolution_bitcast_fusion.3
  756.3 68.0 %reduce-scatter.11.cloned.1.call-done = f32[1,16,2048]{2,1,0:T(8,128)} async-done(((f32[1,256,2048]{2,1,0:T(8,128)}), f32[1,16,2048]{2,1,0:T(8,128)}) %reduce-scatter.11.cloned.1.call-update) | async-done | bytes 131088 | tf_op jit(solution)/shard_map/reduce_scatter | solution.py:151
  (171 shorter events, 30.1 us)
Async XLA Ops:
  7.2 390.8 %copy-start = (bf16[512,2048]{1,0:T(8,128)(2,1)S(1)}, bf16[512,2048]{1,0:T(8,128)(2,1)}, u32[]{:S(2)}) copy-start(bf16[512,2048]{1,0:T(8,128)(2,1)} %param.13) | copy-start | bytes 6291460
  7.2 63.1 %copy-start.4 = (bf16[2048,64]{0,1:T(8,128)(2,1)S(1)}, bf16[2048,64]{0,1:T(8,128)(2,1)}, u32[]{:S(2)}) copy-start(bf16[2048,64]{0,1:T(8,128)(2,1)} %param.12) | copy-start | bytes 786436
  7.2 61.3 %all-gather.7.cloned.1.call-start = ((), (), s32[]{:S(2)}) async-start(), calls=%async_computation.19 | async-start | bytes 1114112 | tf_op jit(solution)/shard_map/all_gather | solution.py:55
  26.0 87.1 %all-gather.5.cloned.1.call-start = ((), (), s32[]{:S(2)}) async-start(), calls=%async_computation.16 | async-start | bytes 1114112 | tf_op jit(solution)/shard_map/all_gather | solution.py:55
  26.7 130.5 %all-gather.11.cloned.1.call-start = ((), (), s32[]{:S(2)}) async-start(), calls=%async_computation.25 | async-start | bytes 1114112 | tf_op jit(solution)/shard_map/all_gather | solution.py:55
  27.4 173.6 %all-gather.9.cloned.1.call-start = ((), (), s32[]{:S(2)}) async-start(), calls=%async_computation.22 | async-start | bytes 1114112 | tf_op jit(solution)/shard_map/all_gather | solution.py:55
  28.0 206.1 %reduce-scatter.13.cloned.1.call-start = ((), (), s32[]{:S(2)}) async-start(), calls=%async_computation.20 | async-start | bytes 737280 | tf_op jit(solution)/shard_map/reduce_scatter | solution.py:66
  74.1 192.6 %reduce-scatter.9.cloned.1.call-start = ((), (), s32[]{:S(2)}) async-start(), calls=%async_computation.17 | async-start | bytes 737280 | tf_op jit(solution)/shard_map/reduce_scatter | solution.py:66
  117.6 1.2 copy-start.2
  118.8 238.4 %reduce-scatter.21.cloned.1.call-start = ((), (), s32[]{:S(2)}) async-start(), calls=%async_computation.26 | async-start | bytes 737280 | tf_op jit(solution)/shard_map/reduce_scatter | solution.py:66
  161.7 1.2 copy-start.3
  162.8 237.2 %reduce-scatter.17.cloned.1.call-start = ((), (), s32[]{:S(2)}) async-start(), calls=%async_computation.23 | async-start | bytes 737280 | tf_op jit(solution)/shard_map/reduce_scatter | solution.py:66
  235.7 32.6 %all-to-all-start.2 = ((bf16[1,16,2,576]{3,2,0,1:T(2,128)(2,1)}), bf16[1,16,2,576]{3,2,0,1:T(2,128)(2,1)S(1)}, u32[]{:S(2)}, u32[]{:S(2)}) async-start(bf16[1,16,2,576]{3,2,0,1:T(2,128)(2,1)} %copy.238), calls=%async_computation.5 | async-start | bytes 81920 | tf_op jit(solution)/shard_map/all_to_all | solution.py:70
  268.3 14.7 %all-to-all-start = ((bf16[1,16,2,576]{3,2,0,1:T(2,128)(2,1)}), bf16[1,16,2,576]{3,2,0,1:T(2,128)(2,1)S(1)}, u32[]{:S(2)}, u32[]{:S(2)}) async-start(bf16[1,16,2,576]{3,2,0,1:T(2,128)(2,1)} %copy.226), calls=%async_computation.1 | async-start | bytes 81920 | tf_op jit(solution)/shard_map/all_to_all | solution.py:70
  353.6 11.0 %all-to-all-start.3 = ((bf16[16,2,512]{2,1,0:T(2,128)(2,1)}), bf16[16,2,512]{2,1,0:T(2,128)(2,1)S(1)}, u32[]{:S(2)}, u32[]{:S(2)}) async-start(bf16[16,2,512]{2,1,0:T(2,128)(2,1)} %reshape.1213), calls=%async_computation.6 | async-start | bytes 65536 | tf_op jit(solution)/shard_map/all_to_all | solution.py:133
  364.7 36.9 %all-to-all-start.6 = ((bf16[1,16,2,576]{3,2,0,1:T(2,128)(2,1)}), bf16[1,16,2,576]{3,2,0,1:T(2,128)(2,1)S(1)}, u32[]{:S(2)}, u32[]{:S(2)}) async-start(bf16[1,16,2,576]{3,2,0,1:T(2,128)(2,1)} %copy.264), calls=%async_computation.13 | async-start | bytes 81920 | tf_op jit(solution)/shard_map/all_to_all | solution.py:70
  368.2 385.3 %reduce-scatter.15.cloned.1.call-start = ((), (), s32[]{:S(2)}) async-start(), calls=%async_computation.21 | async-start | bytes 2228224 | tf_op jit(solution)/shard_map/reduce_scatter | solution.py:151
  401.6 14.8 %all-to-all-start.4 = ((bf16[1,16,2,576]{3,2,0,1:T(2,128)(2,1)}), bf16[1,16,2,576]{3,2,0,1:T(2,128)(2,1)S(1)}, u32[]{:S(2)}, u32[]{:S(2)}) async-start(bf16[1,16,2,576]{3,2,0,1:T(2,128)(2,1)} %copy.251), calls=%async_computation.9 | async-start | bytes 81920 | tf_op jit(solution)/shard_map/all_to_all | solution.py:70
  408.8 345.7 %reduce-scatter.23.cloned.1.call-start = ((), (), s32[]{:S(2)}) async-start(), calls=%async_computation.27 | async-start | bytes 2228224 | tf_op jit(solution)/shard_map/reduce_scatter | solution.py:151
  416.5 6.6 copy-start.1
  528.9 226.5 %reduce-scatter.19.cloned.1.call-start = ((), (), s32[]{:S(2)}) async-start(), calls=%async_computation.24 | async-start | bytes 2228224 | tf_op jit(solution)/shard_map/reduce_scatter | solution.py:151
  641.1 183.2 %reduce-scatter.11.cloned.1.call-start = ((), (), s32[]{:S(2)}) async-start(), calls=%async_computation.18 | async-start | bytes 2228224 | tf_op jit(solution)/shard_map/reduce_scatter | solution.py:151
Sparse Core Ops, SparseCore 0:
  26.1 42.3 all-gather.6
  71.2 41.8 all-gather.4
  115.3 41.8 all-gather.10
  159.2 41.8 all-gather.8
  203.3 30.8 reduce-scatter.12
  236.4 30.2 reduce-scatter.8
  269.1 30.2 reduce-scatter.20
  301.8 30.5 reduce-scatter.16
  400.2 75.4 reduce-scatter.14
  529.0 71.2 reduce-scatter.22
  641.2 71.4 reduce-scatter.18
  752.9 71.2 reduce-scatter.10
where the time goes:
time: 842 us; the launch traced here: 833 us
  waiting for transfers between devices  297 us (35%)
  other arithmetic  202 us (24%)
  local copies, waits for them, and re-layouts  127 us (15%)
  blocking collectives  99 us (12%)
  matrix products  63.4 us (8%)
  starting transfers between devices  29 us (3%)
  between operations  15.4 us (2%)
    unnamed x4, other arithmetic  186 us
    all_gather x4, waiting for transfers between devices, local(): shard_piece = lax.all_gather(normed, 'wide', axis=1, tiled=True)  156 us
    reduce_scatter x4, waiting for transfers between devices, local(): lax.psum_scatter(partials, 'wide', scatter_dimension=1, tiled=True)  68 us
    all_gather x4, blocking collectives, local(): lax.all_gather(by_heads, 'narrow', axis=2, tiled=True)  51.7 us
    reduce_scatter x4, waiting for transfers between devices, local(): lax.psum_scatter(split_terms, 'narrow', scatter_dimension=2, tiled=True)  51.6 us
    unnamed x25, local copies, waits for them, and re-layouts  51.4 us
    all_to_all x3, blocking collectives, local(): lax.all_to_all(attended_heads.reshape(count_steps, 1, rows_dev, HQ * HD),...  32.3 us
    all_to_all x4, local copies, waits for them, and re-layouts, local(): lax.all_to_all(attended_heads.reshape(count_steps, 1, rows_dev, HQ * HD),...  32.3 us
  transfers between devices with their start and end apart: 17, of which 10 were waited for; matrix products, arithmetic and copies ran while one was open for 46% of the time, Pallas kernels for 0%

commit v1 on v0

--- a/solution.py
+++ b/solution.py
@@ -1,13 +1,28 @@
+import functools
 import jax
 import jax.numpy as jnp
 from jax import lax
 from jax.sharding import PartitionSpec as P
+from jax.lax import all_to_all, axis_size
 
 D = 16384
 HQ = 64
 KVH = 4
 HD = 128
 STEPS = 4
+
+
+def remake_the_loops(u, row_axis):
+    w1 = jnp.concatenate(
+        all_to_all(
+            jnp.stack([u] * axis_size(row_axis), 0), axis_name=row_axis, split_axis=0, concat_axis=0
+        ),
+        1,
+    )
+    return w1
+
+
+cut_the_notes = functools.partial(remake_the_loops, row_axis="wide")
 
 
 def rotate(values, rotary_pos):
@@ -52,7 +67,7 @@
         normed = (row_values * inv_rms[..., None] * norm_gain.astype(jnp.float32)).astype(
             jnp.bfloat16
         )
-        shard_piece = lax.all_gather(normed, "wide", axis=1, tiled=True)
+        shard_piece = cut_the_notes(normed)
         first_part = jnp.einsum(
             "trd,dc->trc", shard_piece, w_query, preferred_element_type=jnp.float32
         )

time: 842 us -> 710 us (0.84)
  waiting for transfers between devices: 297 us -> 126 us
  blocking collectives: 99 us -> 142 us
    all_gather x4 -> x0, waiting for transfers between devices: 156 us -> none  [local(): shard_piece = lax.all_gather(normed, 'wide', axis=1, tiled=True)]
    reduce_scatter x4, waiting for transfers between devices: 51.6 us -> 0.08 us  [local(): lax.psum_scatter(split_terms, 'narrow', scatter_dimension=2, tiled=True)]
    all_to_all x0 -> x1, blocking collectives: none -> 22.8 us  [remake_the_loops(): all_to_all(jnp.stack([u] * axis_size(row_axis), 0), axis_name=row_axis, s...]
    all_to_all x1 -> x3, waiting for transfers between devices: 5.97 us -> 28.5 us  [remake_the_loops(): all_to_all(jnp.stack([u] * axis_size(row_axis), 0), axis_name=row_axis, s...]
    all_to_all x4, waiting for transfers between devices: 14.2 us -> 27.8 us  [local(): lax.all_to_all(summed, 'wide', split_axis=1, concat_axis=3, tiled=True)]
    all_to_all x3 -> x4, blocking collectives: 32.3 us -> 43.6 us  [local(): lax.all_to_all(attended_heads.reshape(count_steps, 1, rows_dev, HQ * HD),...]
    all_to_all x4, starting transfers between devices: 24.6 us -> 14 us  [local(): lax.all_to_all(summed, 'wide', split_axis=1, concat_axis=3, tiled=True)]
    all_gather x4, blocking collectives: 51.7 us -> 61 us  [local(): lax.all_gather(by_heads, 'narrow', axis=2, tiled=True)]
  transfers between devices with their start and end apart: 17 -> 15, of which waited for: 10 -> 8; matrix products, arithmetic and copies ran while one was open for 46% -> 55% of each run, Pallas kernels for 0% -> 0%
where the time goes in v1:
time: 710 us; the launch traced here: 700 us
  other arithmetic  202 us (28%)
  blocking collectives  142 us (20%)
  local copies, waits for them, and re-layouts  130 us (18%)
  waiting for transfers between devices  126 us (18%)
  matrix products  57.4 us (8%)
  starting transfers between devices  27.1 us (4%)
  between operations  15.4 us (2%)
    unnamed x4, other arithmetic  186 us
    reduce_scatter x4, waiting for transfers between devices, local(): lax.psum_scatter(partials, 'wide', scatter_dimension=1, tiled=True)  69.8 us
    all_gather x4, blocking collectives, local(): lax.all_gather(by_heads, 'narrow', axis=2, tiled=True)  61 us
    unnamed x35, local copies, waits for them, and re-layouts  51.5 us
    all_to_all x4, blocking collectives, local(): lax.all_to_all(attended_heads.reshape(count_steps, 1, rows_dev, HQ * HD),...  43.6 us
    all_to_all x4, local copies, waits for them, and re-layouts, local(): lax.all_to_all(attended_heads.reshape(count_steps, 1, rows_dev, HQ * HD),...  32.3 us
    all_to_all x3, waiting for transfers between devices, remake_the_loops(): all_to_all(jnp.stack([u] * axis_size(row_axis), 0), axis_name=row_axis, s...  28.5 us
    all_to_all x4, waiting for transfers between devices, local(): lax.all_to_all(summed, 'wide', split_axis=1, concat_axis=3, tiled=True)  27.8 us
  transfers between devices with their start and end apart: 15, of which 8 were waited for; matrix products, arithmetic and copies ran while one was open for 55% of the time, Pallas kernels for 0%

profile of v1, /device:TPU:0, one launch (start us, length us, event | category | flops | bytes accessed | tf_op | source)
XLA Modules:
  0.0 700.3 jit_solution(12119445296841284807)
XLA Ops:
  7.2 1.3 fusion.122
  9.2 15.0 %all-reduce = (f32[1,16]{1,0:T(1,128)S(1)}, f32[1,16]{1,0:T(1,128)S(1)}, f32[1,16]{1,0:T(1,128)S(1)}, f32[1,16]{1,0:T(1,128)S(1)}) all-reduce(f32[1,16]{1,0:T(1,128)S(1)} %bitcast.410, f32[1,16]{1,0:T(1,128)S(1)} %bitcast.411, f32[1,16]{1,0:T(1,128)S(1)} %bitcast.409, ...), channel_id=1, replica_groups=mesh['wide'=16,'narrow'=8] {'narrow'}, use_global_device_ids=true, to_apply=%region_23.24 | all-reduce | flops 64 | bytes 512 | tf_op jit(solution)/shard_map/psum | solution.py:65
  25.3 22.8 %all_to_all.140 = bf16[16,1,16,2048]{3,2,1,0:T(8,128)(2,1)} all-to-all(bf16[16,1,16,2048]{3,2,1,0:T(8,128)(2,1)S(1)} %stack.8), channel_id=1, replica_groups=mesh['wide'=16,'narrow'=8] {'wide'}, dimensions={0} | all-to-all | bytes 2097152 | tf_op jit(solution)/shard_map/all_to_all | solution.py:17
  48.1 1.1 stack.9
  49.2 3.8 all-to-all-start.3
  53.1 2.0 copy.234
  57.5 9.8 %all-to-all-done.3 = bf16[16,1,16,2048]{3,2,1,0:T(8,128)(2,1)S(1)} async-done(((bf16[16,1,16,2048]{3,2,1,0:T(8,128)(2,1)}), bf16[16,1,16,2048]{3,2,1,0:T(8,128)(2,1)S(1)}, u32[]{:S(2)}, u32[]{:S(2)}) %all-to-all-start.3) | async-done | bytes 1048608 | tf_op jit(solution)/shard_map/all_to_all | solution.py:17
  67.3 1.2 stack.10
  68.7 3.7 all-to-all-start.6
  72.4 2.0 copy.247
  77.0 9.1 %all-to-all-done.6 = bf16[16,1,16,2048]{3,2,1,0:T(8,128)(2,1)S(1)} async-done(((bf16[16,1,16,2048]{3,2,1,0:T(8,128)(2,1)}), bf16[16,1,16,2048]{3,2,1,0:T(8,128)(2,1)S(1)}, u32[]{:S(2)}, u32[]{:S(2)}) %all-to-all-start.6) | async-done | bytes 1048608 | tf_op jit(solution)/shard_map/all_to_all | solution.py:17
  86.1 1.2 stack.11
  87.3 4.3 all-to-all-start.9
  95.4 9.6 %all-to-all-done.9 = bf16[16,1,16,2048]{3,2,1,0:T(8,128)(2,1)} async-done(((bf16[16,1,16,2048]{3,2,1,0:T(8,128)(2,1)}), bf16[16,1,16,2048]{3,2,1,0:T(8,128)(2,1)}, u32[]{:S(2)}, u32[]{:S(2)}) %all-to-all-start.9) | async-done | bytes 1048608 | tf_op jit(solution)/shard_map/all_to_all | solution.py:17
  105.0 2.0 copy.275
  109.8 3.5 all-to-all-start.1
  114.8 6.1 all-to-all-done.1
  121.5 5.8 fusion.195
  127.9 4.8 fusion.96
  132.7 6.8 copy.243
  140.0 46.5 %reduce.43 = bf16[8192,2]{1,0:T(8,128)(2,1)} reduce(bf16[8192,1,1,2]{3,2,1,0:T(2,128)(2,1)} %bitcast.352, bf16[]{:T(256)} %broadcast.367), dimensions={1,2}, to_apply=%bitcast.288.reduce_sub_computation | reduce | bytes 65538
  186.6 4.2 reshape.1239
  190.8 10.7 %all_to_all.141 = bf16[16,2,512]{2,1,0:T(2,128)(2,1)S(1)} all-to-all(bf16[16,2,512]{2,1,0:T(2,128)(2,1)S(1)} %reshape.1239), channel_id=1, replica_groups=mesh['wide'=16,'narrow'=8] {'wide'}, dimensions={0} | all-to-all | bytes 65536 | tf_op jit(solution)/shard_map/all_to_all | solution.py:148
  201.5 8.4 %reshape.1240 = bf16[8192,1,1,2]{3,2,1,0:T(2,128)(2,1)} reshape(bf16[16,2,512]{2,1,0:T(2,128)(2,1)S(1)} %all_to_all.141) | data formatting | bytes 65536
  209.9 8.1 %copy.244 = bf16[1,1,2,8192]{3,2,1,0:T(2,128)(2,1)S(1)} copy(bf16[1,1,2,8192]{2,1,0,3:T(2,128)(2,1)} %bitcast.354) | data formatting | bytes 65536 | tf_op jit(solution)/shard_map/all_to_all | solution.py:148
  218.0 22.5 %all_gather.12 = bf16[1,16,8,2,512]{4,1,3,0,2:T(8,128)(2,1)S(1)} all-gather(bf16[1,16,1,2,512]{4,1,3,0,2:T(8,128)(2,1)S(1)} %bitcast.400), channel_id=1, replica_groups=mesh['wide'=16,'narrow'=8] {'narrow'}, dimensions={2}, use_global_device_ids=true | all-gather | bytes 294912 | tf_op jit(solution)/shard_map/all_gather | solution.py:158
  240.9 2.0 convolution_bitcast_fusion.3
  244.5 3.5 all-to-all-start.4
  248.5 7.1 %all-to-all-done.4 = bf16[1,16,2,576]{3,2,0,1:T(2,128)(2,1)S(1)} async-done(((bf16[1,16,2,576]{3,2,0,1:T(2,128)(2,1)}), bf16[1,16,2,576]{3,2,0,1:T(2,128)(2,1)S(1)}, u32[]{:S(2)}, u32[]{:S(2)}) %all-to-all-start.4) | async-done | bytes 36896 | tf_op jit(solution)/shard_map/all_to_all | solution.py:85
  256.3 5.8 fusion.193
  262.6 4.9 fusion.75
  267.8 6.8 copy.257
  274.6 46.6 %reduce.42 = bf16[8192,2]{1,0:T(8,128)(2,1)} reduce(bf16[8192,1,1,2]{3,2,1,0:T(2,128)(2,1)} %bitcast.355, bf16[]{:T(256)} %broadcast.367), dimensions={1,2}, to_apply=%bitcast.286.reduce_sub_computation | reduce | bytes 65538
  321.1 4.2 reshape.1237
  325.3 11.0 %all_to_all.142 = bf16[16,2,512]{2,1,0:T(2,128)(2,1)S(1)} all-to-all(bf16[16,2,512]{2,1,0:T(2,128)(2,1)S(1)} %reshape.1237), channel_id=1, replica_groups=mesh['wide'=16,'narrow'=8] {'wide'}, dimensions={0} | all-to-all | bytes 65536 | tf_op jit(solution)/shard_map/all_to_all | solution.py:148
  336.3 8.4 %reshape.1238 = bf16[8192,1,1,2]{3,2,1,0:T(2,128)(2,1)} reshape(bf16[16,2,512]{2,1,0:T(2,128)(2,1)S(1)} %all_to_all.142) | data formatting | bytes 65536
  344.7 8.1 %copy.258 = bf16[1,1,2,8192]{3,2,1,0:T(2,128)(2,1)S(1)} copy(bf16[1,1,2,8192]{2,1,0,3:T(2,128)(2,1)} %bitcast.356) | data formatting | bytes 65536 | tf_op jit(solution)/shard_map/all_to_all | solution.py:148
  352.8 12.8 %all_gather.13 = bf16[1,16,8,2,512]{4,1,3,0,2:T(8,128)(2,1)S(1)} all-gather(bf16[1,16,1,2,512]{4,1,3,0,2:T(8,128)(2,1)S(1)} %bitcast.401), channel_id=1, replica_groups=mesh['wide'=16,'narrow'=8] {'narrow'}, dimensions={2}, use_global_device_ids=true | all-gather | bytes 294912 | tf_op jit(solution)/shard_map/all_gather | solution.py:158
  366.0 2.1 convolution_bitcast_fusion.2
  369.6 3.5 all-to-all-start.7
  373.4 7.3 %all-to-all-done.7 = bf16[1,16,2,576]{3,2,0,1:T(2,128)(2,1)S(1)} async-done(((bf16[1,16,2,576]{3,2,0,1:T(2,128)(2,1)}), bf16[1,16,2,576]{3,2,0,1:T(2,128)(2,1)S(1)}, u32[]{:S(2)}, u32[]{:S(2)}) %all-to-all-start.7) | async-done | bytes 36896 | tf_op jit(solution)/shard_map/all_to_all | solution.py:85
  381.4 5.8 fusion.191
  387.7 4.9 fusion.78
  392.8 6.8 copy.271
  399.6 46.6 %reduce.41 = bf16[8192,2]{1,0:T(8,128)(2,1)} reduce(bf16[8192,1,1,2]{3,2,1,0:T(2,128)(2,1)} %bitcast.357, bf16[]{:T(256)} %broadcast.367), dimensions={1,2}, to_apply=%bitcast.284.reduce_sub_computation | reduce | bytes 65538
  446.2 4.2 reshape.1235
  450.4 11.0 %all_to_all.143 = bf16[16,2,512]{2,1,0:T(2,128)(2,1)S(1)} all-to-all(bf16[16,2,512]{2,1,0:T(2,128)(2,1)S(1)} %reshape.1235), channel_id=1, replica_groups=mesh['wide'=16,'narrow'=8] {'wide'}, dimensions={0} | all-to-all | bytes 65536 | tf_op jit(solution)/shard_map/all_to_all | solution.py:148
  461.4 8.4 %reshape.1236 = bf16[8192,1,1,2]{3,2,1,0:T(2,128)(2,1)} reshape(bf16[16,2,512]{2,1,0:T(2,128)(2,1)S(1)} %all_to_all.143) | data formatting | bytes 65536
  469.8 8.1 %copy.272 = bf16[1,1,2,8192]{3,2,1,0:T(2,128)(2,1)S(1)} copy(bf16[1,1,2,8192]{2,1,0,3:T(2,128)(2,1)} %bitcast.358) | data formatting | bytes 65536 | tf_op jit(solution)/shard_map/all_to_all | solution.py:148
  477.9 12.8 %all_gather.14 = bf16[1,16,8,2,512]{4,1,3,0,2:T(8,128)(2,1)S(1)} all-gather(bf16[1,16,1,2,512]{4,1,3,0,2:T(8,128)(2,1)S(1)} %bitcast.402), channel_id=1, replica_groups=mesh['wide'=16,'narrow'=8] {'narrow'}, dimensions={2}, use_global_device_ids=true | all-gather | bytes 294912 | tf_op jit(solution)/shard_map/all_gather | solution.py:158
  491.1 2.1 convolution_bitcast_fusion.1
  494.8 3.5 all-to-all-start.10
  498.6 7.3 %all-to-all-done.10 = bf16[1,16,2,576]{3,2,0,1:T(2,128)(2,1)S(1)} async-done(((bf16[1,16,2,576]{3,2,0,1:T(2,128)(2,1)}), bf16[1,16,2,576]{3,2,0,1:T(2,128)(2,1)S(1)}, u32[]{:S(2)}, u32[]{:S(2)}) %all-to-all-start.10) | async-done | bytes 36896 | tf_op jit(solution)/shard_map/all_to_all | solution.py:85
  506.6 5.8 fusion.189
  512.9 4.9 fusion.81
  518.0 6.8 copy.285
  524.8 46.5 %reduce.40 = bf16[8192,2]{1,0:T(8,128)(2,1)} reduce(bf16[8192,1,1,2]{3,2,1,0:T(2,128)(2,1)} %bitcast.353, bf16[]{:T(256)} %broadcast.367), dimensions={1,2}, to_apply=%bitcast.282.reduce_sub_computation | reduce | bytes 65538
  571.3 4.2 reshape.1233
  575.5 10.9 %all_to_all.144 = bf16[16,2,512]{2,1,0:T(2,128)(2,1)S(1)} all-to-all(bf16[16,2,512]{2,1,0:T(2,128)(2,1)S(1)} %reshape.1233), channel_id=1, replica_groups=mesh['wide'=16,'narrow'=8] {'wide'}, dimensions={0} | all-to-all | bytes 65536 | tf_op jit(solution)/shard_map/all_to_all | solution.py:148
  586.5 8.4 %reshape.1234 = bf16[8192,1,1,2]{3,2,1,0:T(2,128)(2,1)} reshape(bf16[16,2,512]{2,1,0:T(2,128)(2,1)S(1)} %all_to_all.144) | data formatting | bytes 65536
  594.8 8.1 %copy.286 = bf16[1,1,2,8192]{3,2,1,0:T(2,128)(2,1)S(1)} copy(bf16[1,1,2,8192]{2,1,0,3:T(2,128)(2,1)} %bitcast.359) | data formatting | bytes 65536 | tf_op jit(solution)/shard_map/all_to_all | solution.py:148
  602.9 12.8 %all_gather.15 = bf16[1,16,8,2,512]{4,1,3,0,2:T(8,128)(2,1)S(1)} all-gather(bf16[1,16,1,2,512]{4,1,3,0,2:T(8,128)(2,1)S(1)} %bitcast.403), channel_id=1, replica_groups=mesh['wide'=16,'narrow'=8] {'narrow'}, dimensions={2}, use_global_device_ids=true | all-gather | bytes 294912 | tf_op jit(solution)/shard_map/all_gather | solution.py:158
  616.2 2.1 convolution_bitcast_fusion
  621.7 69.7 %reduce-scatter.23.cloned.1.call-done = f32[1,16,2048]{2,1,0:T(8,128)} async-done(((f32[1,256,2048]{2,1,0:T(8,128)}), f32[1,16,2048]{2,1,0:T(8,128)}) %reduce-scatter.23.cloned.1.call-update) | async-done | bytes 131088 | tf_op jit(solution)/shard_map/reduce_scatter | solution.py:166
  (183 shorter events, 33.2 us)
Async XLA Ops:
  7.2 233.7 %copy-start = (bf16[512,2048]{1,0:T(8,128)(2,1)S(1)}, bf16[512,2048]{1,0:T(8,128)(2,1)}, u32[]{:S(2)}) copy-start(bf16[512,2048]{1,0:T(8,128)(2,1)} %param.13) | copy-start | bytes 6291460
  49.2 5.8 copy-start.2
  49.2 18.1 %all-to-all-start.3 = ((bf16[16,1,16,2048]{3,2,1,0:T(8,128)(2,1)}), bf16[16,1,16,2048]{3,2,1,0:T(8,128)(2,1)S(1)}, u32[]{:S(2)}, u32[]{:S(2)}) async-start(bf16[16,1,16,2048]{3,2,1,0:T(8,128)(2,1)} %stack.9), calls=%async_computation.5 | async-start | bytes 2097152 | tf_op jit(solution)/shard_map/all_to_all | solution.py:17
  53.0 55.3 %reduce-scatter.9.cloned.1.call-start = ((), (), s32[]{:S(2)}) async-start(), calls=%async_computation.20 | async-start | bytes 737280 | tf_op jit(solution)/shard_map/reduce_scatter | solution.py:81
  53.1 2.5 copy-start.6
  67.3 1.4 copy-start.1
  68.7 17.4 %all-to-all-start.6 = ((bf16[16,1,16,2048]{3,2,1,0:T(8,128)(2,1)}), bf16[16,1,16,2048]{3,2,1,0:T(8,128)(2,1)S(1)}, u32[]{:S(2)}, u32[]{:S(2)}) async-start(bf16[16,1,16,2048]{3,2,1,0:T(8,128)(2,1)} %stack.10), calls=%async_computation.10 | async-start | bytes 2097152 | tf_op jit(solution)/shard_map/all_to_all | solution.py:17
  72.4 170.6 %reduce-scatter.13.cloned.1.call-start = ((), (), s32[]{:S(2)}) async-start(), calls=%async_computation.22 | async-start | bytes 737280 | tf_op jit(solution)/shard_map/reduce_scatter | solution.py:81
  72.4 2.5 copy-start.7
  75.7 1.2 copy-start.4
  75.7 1.3 copy-start.5
  87.3 17.7 %all-to-all-start.9 = ((bf16[16,1,16,2048]{3,2,1,0:T(8,128)(2,1)}), bf16[16,1,16,2048]{3,2,1,0:T(8,128)(2,1)}, u32[]{:S(2)}, u32[]{:S(2)}) async-start(bf16[16,1,16,2048]{3,2,1,0:T(8,128)(2,1)} %stack.11), calls=%async_computation.15 | async-start | bytes 2097152 | tf_op jit(solution)/shard_map/all_to_all | solution.py:17
  91.6 276.5 %reduce-scatter.17.cloned.1.call-start = ((), (), s32[]{:S(2)}) async-start(), calls=%async_computation.24 | async-start | bytes 737280 | tf_op jit(solution)/shard_map/reduce_scatter | solution.py:81
  91.7 1.6 copy-start.8
  105.0 2.5 copy-start.9
  109.8 11.1 %all-to-all-start.1 = ((bf16[1,16,2,576]{3,2,0,1:T(2,128)(2,1)}), bf16[1,16,2,576]{3,2,0,1:T(2,128)(2,1)S(1)}, u32[]{:S(2)}, u32[]{:S(2)}) async-start(bf16[1,16,2,576]{3,2,0,1:T(2,128)(2,1)} %copy.239), calls=%async_computation.2 | async-start | bytes 81920 | tf_op jit(solution)/shard_map/all_to_all | solution.py:85
  113.3 379.9 %reduce-scatter.21.cloned.1.call-start = ((), (), s32[]{:S(2)}) async-start(), calls=%async_computation.26 | async-start | bytes 737280 | tf_op jit(solution)/shard_map/reduce_scatter | solution.py:81
  114.5 504.4 %reduce-scatter.11.cloned.1.call-start = ((), (), s32[]{:S(2)}) async-start(), calls=%async_computation.21 | async-start | bytes 2228224 | tf_op jit(solution)/shard_map/reduce_scatter | solution.py:166
  244.5 11.1 %all-to-all-start.4 = ((bf16[1,16,2,576]{3,2,0,1:T(2,128)(2,1)}), bf16[1,16,2,576]{3,2,0,1:T(2,128)(2,1)S(1)}, u32[]{:S(2)}, u32[]{:S(2)}) async-start(bf16[1,16,2,576]{3,2,0,1:T(2,128)(2,1)} %copy.252), calls=%async_computation.7 | async-start | bytes 81920 | tf_op jit(solution)/shard_map/all_to_all | solution.py:85
  248.0 371.8 %reduce-scatter.15.cloned.1.call-start = ((), (), s32[]{:S(2)}) async-start(), calls=%async_computation.23 | async-start | bytes 2228224 | tf_op jit(solution)/shard_map/reduce_scatter | solution.py:166
  369.6 11.1 %all-to-all-start.7 = ((bf16[1,16,2,576]{3,2,0,1:T(2,128)(2,1)}), bf16[1,16,2,576]{3,2,0,1:T(2,128)(2,1)S(1)}, u32[]{:S(2)}, u32[]{:S(2)}) async-start(bf16[1,16,2,576]{3,2,0,1:T(2,128)(2,1)} %copy.266), calls=%async_computation.12 | async-start | bytes 81920 | tf_op jit(solution)/shard_map/all_to_all | solution.py:85
  373.1 247.6 %reduce-scatter.19.cloned.1.call-start = ((), (), s32[]{:S(2)}) async-start(), calls=%async_computation.25 | async-start | bytes 2228224 | tf_op jit(solution)/shard_map/reduce_scatter | solution.py:166
  494.8 11.1 %all-to-all-start.10 = ((bf16[1,16,2,576]{3,2,0,1:T(2,128)(2,1)}), bf16[1,16,2,576]{3,2,0,1:T(2,128)(2,1)S(1)}, u32[]{:S(2)}, u32[]{:S(2)}) async-start(bf16[1,16,2,576]{3,2,0,1:T(2,128)(2,1)} %copy.280), calls=%async_computation.17 | async-start | bytes 81920 | tf_op jit(solution)/shard_map/all_to_all | solution.py:85
  498.3 193.1 %reduce-scatter.23.cloned.1.call-start = ((), (), s32[]{:S(2)}) async-start(), calls=%async_computation.27 | async-start | bytes 2228224 | tf_op jit(solution)/shard_map/reduce_scatter | solution.py:166
  506.0 6.4 copy-start.3
Sparse Core Ops, SparseCore 0:
  57.6 33.2 reduce-scatter.8
  93.3 31.1 reduce-scatter.12
  126.9 30.1 reduce-scatter.16
  159.3 30.3 reduce-scatter.20
  243.0 73.0 reduce-scatter.10
  368.2 73.0 reduce-scatter.14
  493.3 72.9 reduce-scatter.18
  618.4 73.0 reduce-scatter.22
